TPU v7x, 256 devices: a whole 4x4x8 slice. The times are simulated.
256 devices in a mesh: sub: 4 (over x), row: 16 (over z, core), col: 4 (over y).
Axes of the slice: x: 4, y: 4, z: 8, core: 2. Of those that a mesh axis runs over, the one named last changes fastest.
Arguments:
- leaf_rhs: bfloat16 [4, 64, 4, 64, 256], P('sub', 'row', 'col'), may hold values from -6 to 6
- leaf_inverse: bfloat16 [4, 64, 4, 256, 256], P('sub', 'row', 'col'), may hold values from -0.5 to 0.5
- coupling: bfloat16 [4, 16, 64, 4, 256, 256], P('sub', 'row', None, 'col'), may hold values from -0.01171875 to 0.01171875
- pattern: int32 [4, 16, 64, 4], P('sub', 'row', None, 'col'), may hold values 0 or 1
- top_rhs: bfloat16 [16, 64, 256], replicated, may hold values from -6 to 6
- top_inverse: bfloat16 [16, 256, 256], replicated, may hold values from -0.5 to 0.5
- top_factor: bfloat16 [16, 16, 256, 256], P('row', 'col'), may hold values from -0.09375 to 0.09375
Outputs:
- leaf_solution: bfloat16 [4, 64, 4, 64, 256], P('sub', 'row', 'col')
- top_solution: bfloat16 [16, 64, 256], P('row')
All inputs are finite; a program needn't handle non-finite values. No bound on the sum of `pattern` on one device may be relied on, other than what follows from the above.
Results may differ from a plain program's by a relative error of at most 0.025.
Values may be sent and summed in bfloat16 or wider, within the bound.
No kernel may reach another device: no remote copies, remote signals or barrier semaphores. Data moves between devices by JAX's collectives and lax.ppermute only.
A program may use at most 128 MiB of HBM per device.

v0:
```python
import jax
import jax.numpy as jnp
from jax import lax
from jax.sharding import PartitionSpec as P


def spread(block, axis, source):
    block = jnp.where(lax.axis_index(axis) == source, block, jnp.zeros_like(block))
    return lax.psum(block, axis)


def local(leaf_rhs, leaf_inverse, coupling, pattern, top_rhs, top_inverse, top_factor):
    own_rhs = leaf_rhs[0, :, 0]
    own_inverse = jnp.tril(leaf_inverse[0, :, 0])
    coupled = coupling[0, :, :, 0]
    weights = pattern[0, :, :, 0].astype(jnp.bfloat16)
    blocks_row = coupled.shape[0]
    rhs_count = own_rhs.shape[1]
    block_size = own_rhs.shape[2]
    total_top = top_rhs.shape[0]
    leaf_forward = jnp.einsum(
        "inb,idb->ind", own_rhs, own_inverse, preferred_element_type=jnp.float32
    ).astype(jnp.bfloat16)
    block_slice = coupled
    weight_slice = weights
    scaled = (
        lax.all_gather(leaf_forward, "row", axis=0, tiled=True)[None]
        * weight_slice[:, :, None, None]
    )
    partial_value = jnp.einsum(
        "ainb,aieb->ane", scaled, block_slice, preferred_element_type=jnp.float32
    )
    updates = lax.psum(partial_value.astype(jnp.bfloat16), ("sub", "col")).astype(jnp.float32)
    row_start = lax.axis_index("row") * blocks_row
    full_row = lax.all_gather(top_factor, "col", axis=1, tiled=True)
    row_ids = row_start + jnp.arange(blocks_row)

    def forward_step(block_id, carried):
        pending, solved = carried
        local_row = jnp.clip(block_id - row_start, 0, blocks_row - 1)
        owner_row = block_id // blocks_row
        residue = (
            top_rhs[block_id].astype(jnp.float32) - updates[local_row] - pending[local_row]
        ).astype(jnp.bfloat16)
        solved_piece = jnp.dot(
            residue, jnp.tril(top_inverse[block_id]).T, preferred_element_type=jnp.float32
        ).astype(jnp.bfloat16)
        solved_piece = spread(solved_piece, "row", owner_row)
        column = lax.dynamic_index_in_dim(full_row, block_id, 1, keepdims=False)
        below = (row_ids > block_id).astype(jnp.float32)
        pending = pending + below[:, None, None] * jnp.einsum(
            "nb,aeb->ane", solved_piece, column, preferred_element_type=jnp.float32
        )
        solved = lax.dynamic_update_index_in_dim(solved, solved_piece, block_id, 0)
        return (pending, solved)

    start_state = (
        jnp.zeros((blocks_row, rhs_count, block_size), jnp.float32),
        jnp.zeros((total_top, rhs_count, block_size), jnp.bfloat16),
    )
    forward_all = lax.fori_loop(0, total_top, forward_step, start_state)[1]

    def backward_step(iteration, solved):
        block_id = total_top - 1 - iteration
        own_rows = lax.dynamic_slice_in_dim(solved, row_start, blocks_row, 0)
        above = (row_ids > block_id).astype(jnp.bfloat16)
        column = lax.dynamic_index_in_dim(full_row, block_id, 1, keepdims=False)
        term = jnp.einsum(
            "ane,aeb->nb",
            own_rows * above[:, None, None],
            column,
            preferred_element_type=jnp.float32,
        )
        summed = lax.psum(term.astype(jnp.bfloat16), "row").astype(jnp.float32)
        residue = (forward_all[block_id].astype(jnp.float32) - summed).astype(jnp.bfloat16)
        solved_piece = jnp.dot(
            residue, jnp.tril(top_inverse[block_id]), preferred_element_type=jnp.float32
        ).astype(jnp.bfloat16)
        return lax.dynamic_update_index_in_dim(solved, solved_piece, block_id, 0)

    solution = lax.fori_loop(
        0, total_top, backward_step, jnp.zeros((total_top, rhs_count, block_size), jnp.bfloat16)
    )
    own_top = lax.dynamic_slice_in_dim(solution, row_start, blocks_row, 0)
    block_slice = coupled
    weight_slice = weights
    scaled = own_top[:, None] * weight_slice[:, :, None, None]
    back_sums = lax.psum_scatter(
        jnp.einsum(
            "aine,aieb->inb", scaled, block_slice, preferred_element_type=jnp.float32
        ).astype(jnp.bfloat16),
        "row",
        scatter_dimension=0,
        tiled=True,
    ).astype(jnp.float32)
    leaf_residue = (leaf_forward.astype(jnp.float32) - back_sums).astype(jnp.bfloat16)
    leaf_result = jnp.einsum(
        "inb,ibd->ind", leaf_residue, own_inverse, preferred_element_type=jnp.float32
    ).astype(jnp.bfloat16)
    return (leaf_result[None, :, None], own_top)


def solution(mesh):
    placed = (
        P("sub", "row", "col", None, None),
        P("sub", "row", "col", None, None),
        P("sub", "row", None, "col", None, None),
        P("sub", "row", None, "col"),
        P(),
        P(),
        P("row", "col", None, None),
    )
    return jax.shard_map(
        local,
        mesh=mesh,
        in_specs=placed,
        out_specs=(P("sub", "row", "col", None, None), P("row", None, None)),
        check_vma=False,
    )
```

profile of v0, /device:TPU:4, one launch (start us, length us, event | category | flops | bytes accessed | tf_op | source)
XLA Modules:
  0.0 1736.7 jit_solution(8568360056786855845)
XLA Ops:
  8.1 2.0 fusion.50
  11.6 41.5 %all-gather.5.cloned.1.call-done = bf16[64,64,256]{2,1,0:T(8,128)(2,1)} async-done(((bf16[4,64,256]{2,1,0:T(8,128)(2,1)}), bf16[64,64,256]{2,1,0:T(8,128)(2,1)}) %all-gather.5.cloned.1.call-update) | async-done | bytes 2097168 | tf_op jit(solution)/shard_map/all_gather | solution.py:27
  53.1 6.7 fusion.62
  59.8 62.8 %psum.35 = bf16[1,64,256]{2,1,0:T(8,128)(2,1)S(1)} all-reduce(bf16[1,64,256]{2,1,0:T(8,128)(2,1)S(1)} %fusion.62), channel_id=1, replica_groups=mesh['sub'=4,'row'=16,'col'=4] {'sub','col'}, use_global_device_ids=true, to_apply=%region_0.1 | all-reduce | flops 16384 | bytes 65536 | tf_op jit(solution)/shard_map/psum | solution.py:33
  122.7 768.0 %while.34 = (s32[]{:T(128)}, f32[1,64,256]{2,1,0:T(8,128)S(1)}, bf16[16,64,256]{2,1,0:T(8,128)(2,1)S(1)}, s32[1]{0:T(128)}, bf16[1,16,256,256]{3,2,1,0:T(8,128)(...) while((s32[]{:T(128)}, f32[1,64,256]{2,1,0:T(8,128)S(1)}, ...), condition=%wide.region_3.4_spmd.clone, body=%wide.region_1.3_spmd.clone.sunk | while | flops 17088520 | bytes 755900 | solution.py:61
  123.8 45.7 %psum.40 = bf16[64,256]{1,0:T(8,128)(2,1)S(1)} all-reduce(bf16[64,256]{1,0:T(8,128)(2,1)S(1)} %fusion.97), channel_id=1, replica_groups=mesh['sub'=4,'row'=16,'col'=4] {'row'}, use_global_device_ids=true, to_apply=%region_2.2 | all-reduce | flops 16384 | bytes 65536 | tf_op jit(solution)/shard_map/while/body/eval_jaxpr/psum | solution.py:9
  169.6 1.1 fusion.98
  171.8 45.7 %psum.40 = bf16[64,256]{1,0:T(8,128)(2,1)S(1)} all-reduce(bf16[64,256]{1,0:T(8,128)(2,1)S(1)} %fusion.97), channel_id=1, replica_groups=mesh['sub'=4,'row'=16,'col'=4] {'row'}, use_global_device_ids=true, to_apply=%region_2.2 | all-reduce | flops 16384 | bytes 65536 | tf_op jit(solution)/shard_map/while/body/eval_jaxpr/psum | solution.py:9
  217.6 1.1 fusion.98
  219.8 45.7 %psum.40 = bf16[64,256]{1,0:T(8,128)(2,1)S(1)} all-reduce(bf16[64,256]{1,0:T(8,128)(2,1)S(1)} %fusion.97), channel_id=1, replica_groups=mesh['sub'=4,'row'=16,'col'=4] {'row'}, use_global_device_ids=true, to_apply=%region_2.2 | all-reduce | flops 16384 | bytes 65536 | tf_op jit(solution)/shard_map/while/body/eval_jaxpr/psum | solution.py:9
  265.6 1.1 fusion.98
  267.8 45.7 %psum.40 = bf16[64,256]{1,0:T(8,128)(2,1)S(1)} all-reduce(bf16[64,256]{1,0:T(8,128)(2,1)S(1)} %fusion.97), channel_id=1, replica_groups=mesh['sub'=4,'row'=16,'col'=4] {'row'}, use_global_device_ids=true, to_apply=%region_2.2 | all-reduce | flops 16384 | bytes 65536 | tf_op jit(solution)/shard_map/while/body/eval_jaxpr/psum | solution.py:9
  313.6 1.1 fusion.98
  315.8 45.7 %psum.40 = bf16[64,256]{1,0:T(8,128)(2,1)S(1)} all-reduce(bf16[64,256]{1,0:T(8,128)(2,1)S(1)} %fusion.97), channel_id=1, replica_groups=mesh['sub'=4,'row'=16,'col'=4] {'row'}, use_global_device_ids=true, to_apply=%region_2.2 | all-reduce | flops 16384 | bytes 65536 | tf_op jit(solution)/shard_map/while/body/eval_jaxpr/psum | solution.py:9
  361.6 1.1 fusion.98
  363.8 45.7 %psum.40 = bf16[64,256]{1,0:T(8,128)(2,1)S(1)} all-reduce(bf16[64,256]{1,0:T(8,128)(2,1)S(1)} %fusion.97), channel_id=1, replica_groups=mesh['sub'=4,'row'=16,'col'=4] {'row'}, use_global_device_ids=true, to_apply=%region_2.2 | all-reduce | flops 16384 | bytes 65536 | tf_op jit(solution)/shard_map/while/body/eval_jaxpr/psum | solution.py:9
  411.8 45.7 %psum.40 = bf16[64,256]{1,0:T(8,128)(2,1)S(1)} all-reduce(bf16[64,256]{1,0:T(8,128)(2,1)S(1)} %fusion.97), channel_id=1, replica_groups=mesh['sub'=4,'row'=16,'col'=4] {'row'}, use_global_device_ids=true, to_apply=%region_2.2 | all-reduce | flops 16384 | bytes 65536 | tf_op jit(solution)/shard_map/while/body/eval_jaxpr/psum | solution.py:9
  459.8 45.7 %psum.40 = bf16[64,256]{1,0:T(8,128)(2,1)S(1)} all-reduce(bf16[64,256]{1,0:T(8,128)(2,1)S(1)} %fusion.97), channel_id=1, replica_groups=mesh['sub'=4,'row'=16,'col'=4] {'row'}, use_global_device_ids=true, to_apply=%region_2.2 | all-reduce | flops 16384 | bytes 65536 | tf_op jit(solution)/shard_map/while/body/eval_jaxpr/psum | solution.py:9
  507.8 45.7 %psum.40 = bf16[64,256]{1,0:T(8,128)(2,1)S(1)} all-reduce(bf16[64,256]{1,0:T(8,128)(2,1)S(1)} %fusion.97), channel_id=1, replica_groups=mesh['sub'=4,'row'=16,'col'=4] {'row'}, use_global_device_ids=true, to_apply=%region_2.2 | all-reduce | flops 16384 | bytes 65536 | tf_op jit(solution)/shard_map/while/body/eval_jaxpr/psum | solution.py:9
  553.6 1.1 fusion.98
  555.8 45.7 %psum.40 = bf16[64,256]{1,0:T(8,128)(2,1)S(1)} all-reduce(bf16[64,256]{1,0:T(8,128)(2,1)S(1)} %fusion.97), channel_id=1, replica_groups=mesh['sub'=4,'row'=16,'col'=4] {'row'}, use_global_device_ids=true, to_apply=%region_2.2 | all-reduce | flops 16384 | bytes 65536 | tf_op jit(solution)/shard_map/while/body/eval_jaxpr/psum | solution.py:9
  603.8 45.7 %psum.40 = bf16[64,256]{1,0:T(8,128)(2,1)S(1)} all-reduce(bf16[64,256]{1,0:T(8,128)(2,1)S(1)} %fusion.97), channel_id=1, replica_groups=mesh['sub'=4,'row'=16,'col'=4] {'row'}, use_global_device_ids=true, to_apply=%region_2.2 | all-reduce | flops 16384 | bytes 65536 | tf_op jit(solution)/shard_map/while/body/eval_jaxpr/psum | solution.py:9
  651.8 45.7 %psum.40 = bf16[64,256]{1,0:T(8,128)(2,1)S(1)} all-reduce(bf16[64,256]{1,0:T(8,128)(2,1)S(1)} %fusion.97), channel_id=1, replica_groups=mesh['sub'=4,'row'=16,'col'=4] {'row'}, use_global_device_ids=true, to_apply=%region_2.2 | all-reduce | flops 16384 | bytes 65536 | tf_op jit(solution)/shard_map/while/body/eval_jaxpr/psum | solution.py:9
  699.8 45.7 %psum.40 = bf16[64,256]{1,0:T(8,128)(2,1)S(1)} all-reduce(bf16[64,256]{1,0:T(8,128)(2,1)S(1)} %fusion.97), channel_id=1, replica_groups=mesh['sub'=4,'row'=16,'col'=4] {'row'}, use_global_device_ids=true, to_apply=%region_2.2 | all-reduce | flops 16384 | bytes 65536 | tf_op jit(solution)/shard_map/while/body/eval_jaxpr/psum | solution.py:9
  747.8 45.7 %psum.40 = bf16[64,256]{1,0:T(8,128)(2,1)S(1)} all-reduce(bf16[64,256]{1,0:T(8,128)(2,1)S(1)} %fusion.97), channel_id=1, replica_groups=mesh['sub'=4,'row'=16,'col'=4] {'row'}, use_global_device_ids=true, to_apply=%region_2.2 | all-reduce | flops 16384 | bytes 65536 | tf_op jit(solution)/shard_map/while/body/eval_jaxpr/psum | solution.py:9
  795.8 45.7 %psum.40 = bf16[64,256]{1,0:T(8,128)(2,1)S(1)} all-reduce(bf16[64,256]{1,0:T(8,128)(2,1)S(1)} %fusion.97), channel_id=1, replica_groups=mesh['sub'=4,'row'=16,'col'=4] {'row'}, use_global_device_ids=true, to_apply=%region_2.2 | all-reduce | flops 16384 | bytes 65536 | tf_op jit(solution)/shard_map/while/body/eval_jaxpr/psum | solution.py:9
  843.8 45.7 %psum.40 = bf16[64,256]{1,0:T(8,128)(2,1)S(1)} all-reduce(bf16[64,256]{1,0:T(8,128)(2,1)S(1)} %fusion.97), channel_id=1, replica_groups=mesh['sub'=4,'row'=16,'col'=4] {'row'}, use_global_device_ids=true, to_apply=%region_2.2 | all-reduce | flops 16384 | bytes 65536 | tf_op jit(solution)/shard_map/while/body/eval_jaxpr/psum | solution.py:9
  889.5 1.1 fusion.98
  890.7 765.6 %while.33 = (s32[]{:T(128)}, bf16[16,64,256]{2,1,0:T(8,128)(2,1)S(1)}, bf16[16,64,256]{2,1,0:T(8,128)(2,1)S(1)}, s32[]{:T(128)}, s32[1]{0:T(128)}, /*index=5*/bf...) while((s32[]{:T(128)}, ...), condition=%wide.region_6.7_spmd, body=%wide.region_4.6_spmd.sunk | while | flops 17039368 | bytes 494251 | solution.py:81
  891.8 45.7 %psum.39 = bf16[64,256]{1,0:T(8,128)(2,1)S(1)} all-reduce(bf16[64,256]{1,0:T(8,128)(2,1)S(1)} %convolution_convert_fusion.6), channel_id=1, replica_groups=mesh['sub'=4,'row'=16,'col'=4] {'row'}, use_global_device_ids=true, to_apply=%region_5.5 | all-reduce | flops 16384 | bytes 65536 | tf_op jit(solution)/shard_map/while/body/eval_jaxpr/psum | solution.py:74
  939.6 45.7 %psum.39 = bf16[64,256]{1,0:T(8,128)(2,1)S(1)} all-reduce(bf16[64,256]{1,0:T(8,128)(2,1)S(1)} %convolution_convert_fusion.6), channel_id=1, replica_groups=mesh['sub'=4,'row'=16,'col'=4] {'row'}, use_global_device_ids=true, to_apply=%region_5.5 | all-reduce | flops 16384 | bytes 65536 | tf_op jit(solution)/shard_map/while/body/eval_jaxpr/psum | solution.py:74
  987.5 45.7 %psum.39 = bf16[64,256]{1,0:T(8,128)(2,1)S(1)} all-reduce(bf16[64,256]{1,0:T(8,128)(2,1)S(1)} %convolution_convert_fusion.6), channel_id=1, replica_groups=mesh['sub'=4,'row'=16,'col'=4] {'row'}, use_global_device_ids=true, to_apply=%region_5.5 | all-reduce | flops 16384 | bytes 65536 | tf_op jit(solution)/shard_map/while/body/eval_jaxpr/psum | solution.py:74
  1035.3 45.7 %psum.39 = bf16[64,256]{1,0:T(8,128)(2,1)S(1)} all-reduce(bf16[64,256]{1,0:T(8,128)(2,1)S(1)} %convolution_convert_fusion.6), channel_id=1, replica_groups=mesh['sub'=4,'row'=16,'col'=4] {'row'}, use_global_device_ids=true, to_apply=%region_5.5 | all-reduce | flops 16384 | bytes 65536 | tf_op jit(solution)/shard_map/while/body/eval_jaxpr/psum | solution.py:74
  1083.2 45.7 %psum.39 = bf16[64,256]{1,0:T(8,128)(2,1)S(1)} all-reduce(bf16[64,256]{1,0:T(8,128)(2,1)S(1)} %convolution_convert_fusion.6), channel_id=1, replica_groups=mesh['sub'=4,'row'=16,'col'=4] {'row'}, use_global_device_ids=true, to_apply=%region_5.5 | all-reduce | flops 16384 | bytes 65536 | tf_op jit(solution)/shard_map/while/body/eval_jaxpr/psum | solution.py:74
  1131.0 45.7 %psum.39 = bf16[64,256]{1,0:T(8,128)(2,1)S(1)} all-reduce(bf16[64,256]{1,0:T(8,128)(2,1)S(1)} %convolution_convert_fusion.6), channel_id=1, replica_groups=mesh['sub'=4,'row'=16,'col'=4] {'row'}, use_global_device_ids=true, to_apply=%region_5.5 | all-reduce | flops 16384 | bytes 65536 | tf_op jit(solution)/shard_map/while/body/eval_jaxpr/psum | solution.py:74
  1178.9 45.7 %psum.39 = bf16[64,256]{1,0:T(8,128)(2,1)S(1)} all-reduce(bf16[64,256]{1,0:T(8,128)(2,1)S(1)} %convolution_convert_fusion.6), channel_id=1, replica_groups=mesh['sub'=4,'row'=16,'col'=4] {'row'}, use_global_device_ids=true, to_apply=%region_5.5 | all-reduce | flops 16384 | bytes 65536 | tf_op jit(solution)/shard_map/while/body/eval_jaxpr/psum | solution.py:74
  1226.7 45.7 %psum.39 = bf16[64,256]{1,0:T(8,128)(2,1)S(1)} all-reduce(bf16[64,256]{1,0:T(8,128)(2,1)S(1)} %convolution_convert_fusion.6), channel_id=1, replica_groups=mesh['sub'=4,'row'=16,'col'=4] {'row'}, use_global_device_ids=true, to_apply=%region_5.5 | all-reduce | flops 16384 | bytes 65536 | tf_op jit(solution)/shard_map/while/body/eval_jaxpr/psum | solution.py:74
  1274.6 45.7 %psum.39 = bf16[64,256]{1,0:T(8,128)(2,1)S(1)} all-reduce(bf16[64,256]{1,0:T(8,128)(2,1)S(1)} %convolution_convert_fusion.6), channel_id=1, replica_groups=mesh['sub'=4,'row'=16,'col'=4] {'row'}, use_global_device_ids=true, to_apply=%region_5.5 | all-reduce | flops 16384 | bytes 65536 | tf_op jit(solution)/shard_map/while/body/eval_jaxpr/psum | solution.py:74
  1322.4 45.7 %psum.39 = bf16[64,256]{1,0:T(8,128)(2,1)S(1)} all-reduce(bf16[64,256]{1,0:T(8,128)(2,1)S(1)} %convolution_convert_fusion.6), channel_id=1, replica_groups=mesh['sub'=4,'row'=16,'col'=4] {'row'}, use_global_device_ids=true, to_apply=%region_5.5 | all-reduce | flops 16384 | bytes 65536 | tf_op jit(solution)/shard_map/while/body/eval_jaxpr/psum | solution.py:74
  1370.3 45.7 %psum.39 = bf16[64,256]{1,0:T(8,128)(2,1)S(1)} all-reduce(bf16[64,256]{1,0:T(8,128)(2,1)S(1)} %convolution_convert_fusion.6), channel_id=1, replica_groups=mesh['sub'=4,'row'=16,'col'=4] {'row'}, use_global_device_ids=true, to_apply=%region_5.5 | all-reduce | flops 16384 | bytes 65536 | tf_op jit(solution)/shard_map/while/body/eval_jaxpr/psum | solution.py:74
  1418.1 45.7 %psum.39 = bf16[64,256]{1,0:T(8,128)(2,1)S(1)} all-reduce(bf16[64,256]{1,0:T(8,128)(2,1)S(1)} %convolution_convert_fusion.6), channel_id=1, replica_groups=mesh['sub'=4,'row'=16,'col'=4] {'row'}, use_global_device_ids=true, to_apply=%region_5.5 | all-reduce | flops 16384 | bytes 65536 | tf_op jit(solution)/shard_map/while/body/eval_jaxpr/psum | solution.py:74
  1466.0 45.7 %psum.39 = bf16[64,256]{1,0:T(8,128)(2,1)S(1)} all-reduce(bf16[64,256]{1,0:T(8,128)(2,1)S(1)} %convolution_convert_fusion.6), channel_id=1, replica_groups=mesh['sub'=4,'row'=16,'col'=4] {'row'}, use_global_device_ids=true, to_apply=%region_5.5 | all-reduce | flops 16384 | bytes 65536 | tf_op jit(solution)/shard_map/while/body/eval_jaxpr/psum | solution.py:74
  1513.8 45.7 %psum.39 = bf16[64,256]{1,0:T(8,128)(2,1)S(1)} all-reduce(bf16[64,256]{1,0:T(8,128)(2,1)S(1)} %convolution_convert_fusion.6), channel_id=1, replica_groups=mesh['sub'=4,'row'=16,'col'=4] {'row'}, use_global_device_ids=true, to_apply=%region_5.5 | all-reduce | flops 16384 | bytes 65536 | tf_op jit(solution)/shard_map/while/body/eval_jaxpr/psum | solution.py:74
  1561.6 45.7 %psum.39 = bf16[64,256]{1,0:T(8,128)(2,1)S(1)} all-reduce(bf16[64,256]{1,0:T(8,128)(2,1)S(1)} %convolution_convert_fusion.6), channel_id=1, replica_groups=mesh['sub'=4,'row'=16,'col'=4] {'row'}, use_global_device_ids=true, to_apply=%region_5.5 | all-reduce | flops 16384 | bytes 65536 | tf_op jit(solution)/shard_map/while/body/eval_jaxpr/psum | solution.py:74
  1609.5 45.7 %psum.39 = bf16[64,256]{1,0:T(8,128)(2,1)S(1)} all-reduce(bf16[64,256]{1,0:T(8,128)(2,1)S(1)} %convolution_convert_fusion.6), channel_id=1, replica_groups=mesh['sub'=4,'row'=16,'col'=4] {'row'}, use_global_device_ids=true, to_apply=%region_5.5 | all-reduce | flops 16384 | bytes 65536 | tf_op jit(solution)/shard_map/while/body/eval_jaxpr/psum | solution.py:74
  1656.3 6.4 fusion.45
  1663.3 65.1 %reduce-scatter.2.cloned.1.call-done = bf16[4,64,256]{2,1,0:T(8,128)(2,1)} async-done(((bf16[64,64,256]{2,1,0:T(8,128)(2,1)}), bf16[4,64,256]{2,1,0:T(8,128)(2,1)}) %reduce-scatter.2.cloned.1.call-update) | async-done | bytes 131088 | tf_op jit(solution)/shard_map/reduce_scatter | solution.py:88
  1728.4 1.8 fusion.51
  (94 shorter events, 64.2 us)
Async XLA Ops:
  7.2 0.9 copy-start
  7.2 45.9 %all-gather.5.cloned.1.call-start = ((), (), s32[]{:S(2)}) async-start(), calls=%async_computation.2 | async-start | bytes 2228224 | tf_op jit(solution)/shard_map/all_gather | solution.py:27
  10.1 112.6 %all-gather.3.cloned.1.call-start = ((), (), s32[]{:S(2)}) async-start(), calls=%async_computation.1 | async-start | bytes 2621440 | tf_op jit(solution)/shard_map/all_gather | solution.py:35
  10.8 1717.5 %reduce-scatter.2.cloned.1.call-start = ((), (), s32[]{:S(2)}) async-start(), calls=%async_computation.3 | async-start | bytes 2228224 | tf_op jit(solution)/shard_map/reduce_scatter | solution.py:88
  1662.7 65.7 %copy-start.1 = (bf16[4,64,256]{2,1,0:T(8,128)(2,1)S(1)}, bf16[4,64,256]{2,1,0:T(8,128)(2,1)}, u32[]{:S(2)}) copy-start(bf16[4,64,256]{2,1,0:T(8,128)(2,1)} %fusion.50) | copy-start | bytes 393220
  1662.7 65.7 %copy-start.2 = (bf16[1,4,1,256,256]{4,3,2,1,0:T(8,128)(2,1)S(1)}, bf16[1,4,1,256,256]{4,3,2,1,0:T(8,128)(2,1)}, u32[]{:S(2)}) copy-start(bf16[1,4,1,256,256]{4,3,2,1,0:T(8,128)(2,1)} %param.12) | copy-start | bytes 1572868
Sparse Core Ops, SparseCore 0:
  10.4 42.6 all-gather.4
  54.9 32.1 all-gather.2
  1662.8 65.5 reduce-scatter.1
where the time goes:
time: 1740 us
  blocking collectives  1530 us (88%)
  waiting for transfers between devices  107 us (6%)
  matrix products  85.4 us (5%)
    psum x16, blocking collectives, backward_step(): summed = lax.psum(term.astype(jnp.bfloat16), 'row').astype(jnp.float32)  732 us
    psum x16, blocking collectives, spread(): return lax.psum(block, axis)  732 us
    reduce_scatter x1, waiting for transfers between devices, local(): lax.psum_scatter(jnp.einsum('aine,aieb->inb', scaled, block_slice, prefer...  65.1 us
    psum x1, blocking collectives, local(): lax.psum(partial_value.astype(jnp.bfloat16), ('sub', 'col'))  62.8 us
    all_gather x1, waiting for transfers between devices, local(): lax.all_gather(leaf_forward, 'row', axis=0, tiled=True)[None]  41.5 us
  transfers between devices with their start and end apart: 3, of which 2 were waited for; matrix products, arithmetic and copies ran while one was open for 0% of the time, Pallas kernels for 0%

commit v1 on v0

--- a/solution.py
+++ b/solution.py
@@ -24,7 +24,9 @@
     block_slice = coupled
     weight_slice = weights
     scaled = (
-        lax.all_gather(leaf_forward, "row", axis=0, tiled=True)[None]
+        jnp.concatenate(
+            lax.all_to_all(jnp.stack([leaf_forward] * lax.axis_size("row")), "row", 0, 0), axis=0
+        )[None]
         * weight_slice[:, :, None, None]
     )
     partial_value = jnp.einsum(

time: 1740 us -> 1760 us (1.011)
    all_to_all x0 -> x1, waiting for transfers between devices: none -> 48.4 us  [local(): lax.all_to_all(jnp.stack([leaf_forward] * lax.axis_size('row')), 'row', 0...]
    all_gather x1 -> x0, waiting for transfers between devices: 41.5 us -> none  [local(): lax.all_gather(leaf_forward, 'row', axis=0, tiled=True)[None]]
where the time goes in v1:
time: 1760 us; the launch traced here: 1750 us
  blocking collectives  1530 us (87%)
  waiting for transfers between devices  115 us (7%)
  matrix products  84.1 us (5%)
    psum x16, blocking collectives, backward_step(): summed = lax.psum(term.astype(jnp.bfloat16), 'row').astype(jnp.float32)  732 us
    psum x16, blocking collectives, spread(): return lax.psum(block, axis)  732 us
    reduce_scatter x1, waiting for transfers between devices, local(): lax.psum_scatter(jnp.einsum('aine,aieb->inb', scaled, block_slice, prefer...  65.5 us
    psum x1, blocking collectives, local(): lax.psum(partial_value.astype(jnp.bfloat16), ('sub', 'col'))  62.8 us
    all_to_all x1, waiting for transfers between devices, local(): lax.all_to_all(jnp.stack([leaf_forward] * lax.axis_size('row')), 'row', 0...  48.4 us
  transfers between devices with their start and end apart: 3, of which 2 were waited for; matrix products, arithmetic and copies ran while one was open for 0% of the time, Pallas kernels for 0%

profile of v1, /device:TPU:4, one launch (start us, length us, event | category | flops | bytes accessed | tf_op | source)
XLA Modules:
  0.0 1752.9 jit_solution(16327709804469332963)
XLA Ops:
  8.1 1.3 fusion.49
  9.4 1.6 stack.2
  11.0 8.7 all-to-all-start
  20.5 48.4 %all-to-all-done = bf16[16,4,64,256]{3,2,1,0:T(8,128)(2,1)S(1)} async-done(((bf16[16,4,64,256]{3,2,1,0:T(8,128)(2,1)}), bf16[16,4,64,256]{3,2,1,0:T(8,128)(2,1)S(1)}, u32[]{:S(2)}, u32[]{:S(2)}) %all-to-all-start) | async-done | bytes 2097184 | tf_op jit(solution)/shard_map/all_to_all | solution.py:28
  69.3 6.0 fusion.57
  75.3 62.8 %psum.35 = bf16[1,64,256]{2,1,0:T(8,128)(2,1)S(1)} all-reduce(bf16[1,64,256]{2,1,0:T(8,128)(2,1)S(1)} %fusion.57), channel_id=1, replica_groups=mesh['sub'=4,'row'=16,'col'=4] {'sub','col'}, use_global_device_ids=true, to_apply=%region_0.1 | all-reduce | flops 16384 | bytes 65536 | tf_op jit(solution)/shard_map/psum | solution.py:35
  138.1 768.0 %while.34 = (s32[]{:T(128)}, f32[1,64,256]{2,1,0:T(8,128)S(1)}, bf16[16,64,256]{2,1,0:T(8,128)(2,1)S(1)}, s32[1]{0:T(128)}, bf16[1,16,256,256]{3,2,1,0:T(8,128)(...) while((s32[]{:T(128)}, f32[1,64,256]{2,1,0:T(8,128)S(1)}, ...), condition=%wide.region_3.4_spmd.clone, body=%wide.region_1.3_spmd.clone.sunk | while | flops 17088520 | bytes 755900 | solution.py:63
  139.3 45.7 %psum.40 = bf16[64,256]{1,0:T(8,128)(2,1)S(1)} all-reduce(bf16[64,256]{1,0:T(8,128)(2,1)S(1)} %fusion.90), channel_id=1, replica_groups=mesh['sub'=4,'row'=16,'col'=4] {'row'}, use_global_device_ids=true, to_apply=%region_2.2 | all-reduce | flops 16384 | bytes 65536 | tf_op jit(solution)/shard_map/while/body/eval_jaxpr/psum | solution.py:9
  185.0 1.1 fusion.91
  187.3 45.7 %psum.40 = bf16[64,256]{1,0:T(8,128)(2,1)S(1)} all-reduce(bf16[64,256]{1,0:T(8,128)(2,1)S(1)} %fusion.90), channel_id=1, replica_groups=mesh['sub'=4,'row'=16,'col'=4] {'row'}, use_global_device_ids=true, to_apply=%region_2.2 | all-reduce | flops 16384 | bytes 65536 | tf_op jit(solution)/shard_map/while/body/eval_jaxpr/psum | solution.py:9
  233.0 1.1 fusion.91
  235.3 45.7 %psum.40 = bf16[64,256]{1,0:T(8,128)(2,1)S(1)} all-reduce(bf16[64,256]{1,0:T(8,128)(2,1)S(1)} %fusion.90), channel_id=1, replica_groups=mesh['sub'=4,'row'=16,'col'=4] {'row'}, use_global_device_ids=true, to_apply=%region_2.2 | all-reduce | flops 16384 | bytes 65536 | tf_op jit(solution)/shard_map/while/body/eval_jaxpr/psum | solution.py:9
  281.0 1.1 fusion.91
  283.3 45.7 %psum.40 = bf16[64,256]{1,0:T(8,128)(2,1)S(1)} all-reduce(bf16[64,256]{1,0:T(8,128)(2,1)S(1)} %fusion.90), channel_id=1, replica_groups=mesh['sub'=4,'row'=16,'col'=4] {'row'}, use_global_device_ids=true, to_apply=%region_2.2 | all-reduce | flops 16384 | bytes 65536 | tf_op jit(solution)/shard_map/while/body/eval_jaxpr/psum | solution.py:9
  329.0 1.1 fusion.91
  331.3 45.7 %psum.40 = bf16[64,256]{1,0:T(8,128)(2,1)S(1)} all-reduce(bf16[64,256]{1,0:T(8,128)(2,1)S(1)} %fusion.90), channel_id=1, replica_groups=mesh['sub'=4,'row'=16,'col'=4] {'row'}, use_global_device_ids=true, to_apply=%region_2.2 | all-reduce | flops 16384 | bytes 65536 | tf_op jit(solution)/shard_map/while/body/eval_jaxpr/psum | solution.py:9
  379.3 45.7 %psum.40 = bf16[64,256]{1,0:T(8,128)(2,1)S(1)} all-reduce(bf16[64,256]{1,0:T(8,128)(2,1)S(1)} %fusion.90), channel_id=1, replica_groups=mesh['sub'=4,'row'=16,'col'=4] {'row'}, use_global_device_ids=true, to_apply=%region_2.2 | all-reduce | flops 16384 | bytes 65536 | tf_op jit(solution)/shard_map/while/body/eval_jaxpr/psum | solution.py:9
  427.3 45.7 %psum.40 = bf16[64,256]{1,0:T(8,128)(2,1)S(1)} all-reduce(bf16[64,256]{1,0:T(8,128)(2,1)S(1)} %fusion.90), channel_id=1, replica_groups=mesh['sub'=4,'row'=16,'col'=4] {'row'}, use_global_device_ids=true, to_apply=%region_2.2 | all-reduce | flops 16384 | bytes 65536 | tf_op jit(solution)/shard_map/while/body/eval_jaxpr/psum | solution.py:9
  473.0 1.1 fusion.91
  475.3 45.7 %psum.40 = bf16[64,256]{1,0:T(8,128)(2,1)S(1)} all-reduce(bf16[64,256]{1,0:T(8,128)(2,1)S(1)} %fusion.90), channel_id=1, replica_groups=mesh['sub'=4,'row'=16,'col'=4] {'row'}, use_global_device_ids=true, to_apply=%region_2.2 | all-reduce | flops 16384 | bytes 65536 | tf_op jit(solution)/shard_map/while/body/eval_jaxpr/psum | solution.py:9
  523.3 45.7 %psum.40 = bf16[64,256]{1,0:T(8,128)(2,1)S(1)} all-reduce(bf16[64,256]{1,0:T(8,128)(2,1)S(1)} %fusion.90), channel_id=1, replica_groups=mesh['sub'=4,'row'=16,'col'=4] {'row'}, use_global_device_ids=true, to_apply=%region_2.2 | all-reduce | flops 16384 | bytes 65536 | tf_op jit(solution)/shard_map/while/body/eval_jaxpr/psum | solution.py:9
  571.3 45.7 %psum.40 = bf16[64,256]{1,0:T(8,128)(2,1)S(1)} all-reduce(bf16[64,256]{1,0:T(8,128)(2,1)S(1)} %fusion.90), channel_id=1, replica_groups=mesh['sub'=4,'row'=16,'col'=4] {'row'}, use_global_device_ids=true, to_apply=%region_2.2 | all-reduce | flops 16384 | bytes 65536 | tf_op jit(solution)/shard_map/while/body/eval_jaxpr/psum | solution.py:9
  619.3 45.7 %psum.40 = bf16[64,256]{1,0:T(8,128)(2,1)S(1)} all-reduce(bf16[64,256]{1,0:T(8,128)(2,1)S(1)} %fusion.90), channel_id=1, replica_groups=mesh['sub'=4,'row'=16,'col'=4] {'row'}, use_global_device_ids=true, to_apply=%region_2.2 | all-reduce | flops 16384 | bytes 65536 | tf_op jit(solution)/shard_map/while/body/eval_jaxpr/psum | solution.py:9
  667.3 45.7 %psum.40 = bf16[64,256]{1,0:T(8,128)(2,1)S(1)} all-reduce(bf16[64,256]{1,0:T(8,128)(2,1)S(1)} %fusion.90), channel_id=1, replica_groups=mesh['sub'=4,'row'=16,'col'=4] {'row'}, use_global_device_ids=true, to_apply=%region_2.2 | all-reduce | flops 16384 | bytes 65536 | tf_op jit(solution)/shard_map/while/body/eval_jaxpr/psum | solution.py:9
  715.3 45.7 %psum.40 = bf16[64,256]{1,0:T(8,128)(2,1)S(1)} all-reduce(bf16[64,256]{1,0:T(8,128)(2,1)S(1)} %fusion.90), channel_id=1, replica_groups=mesh['sub'=4,'row'=16,'col'=4] {'row'}, use_global_device_ids=true, to_apply=%region_2.2 | all-reduce | flops 16384 | bytes 65536 | tf_op jit(solution)/shard_map/while/body/eval_jaxpr/psum | solution.py:9
  763.3 45.7 %psum.40 = bf16[64,256]{1,0:T(8,128)(2,1)S(1)} all-reduce(bf16[64,256]{1,0:T(8,128)(2,1)S(1)} %fusion.90), channel_id=1, replica_groups=mesh['sub'=4,'row'=16,'col'=4] {'row'}, use_global_device_ids=true, to_apply=%region_2.2 | all-reduce | flops 16384 | bytes 65536 | tf_op jit(solution)/shard_map/while/body/eval_jaxpr/psum | solution.py:9
  811.3 45.7 %psum.40 = bf16[64,256]{1,0:T(8,128)(2,1)S(1)} all-reduce(bf16[64,256]{1,0:T(8,128)(2,1)S(1)} %fusion.90), channel_id=1, replica_groups=mesh['sub'=4,'row'=16,'col'=4] {'row'}, use_global_device_ids=true, to_apply=%region_2.2 | all-reduce | flops 16384 | bytes 65536 | tf_op jit(solution)/shard_map/while/body/eval_jaxpr/psum | solution.py:9
  859.3 45.7 %psum.40 = bf16[64,256]{1,0:T(8,128)(2,1)S(1)} all-reduce(bf16[64,256]{1,0:T(8,128)(2,1)S(1)} %fusion.90), channel_id=1, replica_groups=mesh['sub'=4,'row'=16,'col'=4] {'row'}, use_global_device_ids=true, to_apply=%region_2.2 | all-reduce | flops 16384 | bytes 65536 | tf_op jit(solution)/shard_map/while/body/eval_jaxpr/psum | solution.py:9
  906.2 765.6 %while.33 = (s32[]{:T(128)}, bf16[16,64,256]{2,1,0:T(8,128)(2,1)S(1)}, bf16[16,64,256]{2,1,0:T(8,128)(2,1)S(1)}, s32[]{:T(128)}, s32[1]{0:T(128)}, /*index=5*/bf...) while((s32[]{:T(128)}, ...), condition=%wide.region_6.7_spmd, body=%wide.region_4.6_spmd.sunk | while | flops 17039368 | bytes 494251 | solution.py:83
  907.3 45.7 %psum.39 = bf16[64,256]{1,0:T(8,128)(2,1)S(1)} all-reduce(bf16[64,256]{1,0:T(8,128)(2,1)S(1)} %convolution_convert_fusion.6), channel_id=1, replica_groups=mesh['sub'=4,'row'=16,'col'=4] {'row'}, use_global_device_ids=true, to_apply=%region_5.5 | all-reduce | flops 16384 | bytes 65536 | tf_op jit(solution)/shard_map/while/body/eval_jaxpr/psum | solution.py:76
  955.1 45.7 %psum.39 = bf16[64,256]{1,0:T(8,128)(2,1)S(1)} all-reduce(bf16[64,256]{1,0:T(8,128)(2,1)S(1)} %convolution_convert_fusion.6), channel_id=1, replica_groups=mesh['sub'=4,'row'=16,'col'=4] {'row'}, use_global_device_ids=true, to_apply=%region_5.5 | all-reduce | flops 16384 | bytes 65536 | tf_op jit(solution)/shard_map/while/body/eval_jaxpr/psum | solution.py:76
  1003.0 45.7 %psum.39 = bf16[64,256]{1,0:T(8,128)(2,1)S(1)} all-reduce(bf16[64,256]{1,0:T(8,128)(2,1)S(1)} %convolution_convert_fusion.6), channel_id=1, replica_groups=mesh['sub'=4,'row'=16,'col'=4] {'row'}, use_global_device_ids=true, to_apply=%region_5.5 | all-reduce | flops 16384 | bytes 65536 | tf_op jit(solution)/shard_map/while/body/eval_jaxpr/psum | solution.py:76
  1050.8 45.7 %psum.39 = bf16[64,256]{1,0:T(8,128)(2,1)S(1)} all-reduce(bf16[64,256]{1,0:T(8,128)(2,1)S(1)} %convolution_convert_fusion.6), channel_id=1, replica_groups=mesh['sub'=4,'row'=16,'col'=4] {'row'}, use_global_device_ids=true, to_apply=%region_5.5 | all-reduce | flops 16384 | bytes 65536 | tf_op jit(solution)/shard_map/while/body/eval_jaxpr/psum | solution.py:76
  1098.7 45.7 %psum.39 = bf16[64,256]{1,0:T(8,128)(2,1)S(1)} all-reduce(bf16[64,256]{1,0:T(8,128)(2,1)S(1)} %convolution_convert_fusion.6), channel_id=1, replica_groups=mesh['sub'=4,'row'=16,'col'=4] {'row'}, use_global_device_ids=true, to_apply=%region_5.5 | all-reduce | flops 16384 | bytes 65536 | tf_op jit(solution)/shard_map/while/body/eval_jaxpr/psum | solution.py:76
  1146.5 45.7 %psum.39 = bf16[64,256]{1,0:T(8,128)(2,1)S(1)} all-reduce(bf16[64,256]{1,0:T(8,128)(2,1)S(1)} %convolution_convert_fusion.6), channel_id=1, replica_groups=mesh['sub'=4,'row'=16,'col'=4] {'row'}, use_global_device_ids=true, to_apply=%region_5.5 | all-reduce | flops 16384 | bytes 65536 | tf_op jit(solution)/shard_map/while/body/eval_jaxpr/psum | solution.py:76
  1194.3 45.7 %psum.39 = bf16[64,256]{1,0:T(8,128)(2,1)S(1)} all-reduce(bf16[64,256]{1,0:T(8,128)(2,1)S(1)} %convolution_convert_fusion.6), channel_id=1, replica_groups=mesh['sub'=4,'row'=16,'col'=4] {'row'}, use_global_device_ids=true, to_apply=%region_5.5 | all-reduce | flops 16384 | bytes 65536 | tf_op jit(solution)/shard_map/while/body/eval_jaxpr/psum | solution.py:76
  1242.2 45.7 %psum.39 = bf16[64,256]{1,0:T(8,128)(2,1)S(1)} all-reduce(bf16[64,256]{1,0:T(8,128)(2,1)S(1)} %convolution_convert_fusion.6), channel_id=1, replica_groups=mesh['sub'=4,'row'=16,'col'=4] {'row'}, use_global_device_ids=true, to_apply=%region_5.5 | all-reduce | flops 16384 | bytes 65536 | tf_op jit(solution)/shard_map/while/body/eval_jaxpr/psum | solution.py:76
  1290.0 45.7 %psum.39 = bf16[64,256]{1,0:T(8,128)(2,1)S(1)} all-reduce(bf16[64,256]{1,0:T(8,128)(2,1)S(1)} %convolution_convert_fusion.6), channel_id=1, replica_groups=mesh['sub'=4,'row'=16,'col'=4] {'row'}, use_global_device_ids=true, to_apply=%region_5.5 | all-reduce | flops 16384 | bytes 65536 | tf_op jit(solution)/shard_map/while/body/eval_jaxpr/psum | solution.py:76
  1337.9 45.7 %psum.39 = bf16[64,256]{1,0:T(8,128)(2,1)S(1)} all-reduce(bf16[64,256]{1,0:T(8,128)(2,1)S(1)} %convolution_convert_fusion.6), channel_id=1, replica_groups=mesh['sub'=4,'row'=16,'col'=4] {'row'}, use_global_device_ids=true, to_apply=%region_5.5 | all-reduce | flops 16384 | bytes 65536 | tf_op jit(solution)/shard_map/while/body/eval_jaxpr/psum | solution.py:76
  1385.7 45.7 %psum.39 = bf16[64,256]{1,0:T(8,128)(2,1)S(1)} all-reduce(bf16[64,256]{1,0:T(8,128)(2,1)S(1)} %convolution_convert_fusion.6), channel_id=1, replica_groups=mesh['sub'=4,'row'=16,'col'=4] {'row'}, use_global_device_ids=true, to_apply=%region_5.5 | all-reduce | flops 16384 | bytes 65536 | tf_op jit(solution)/shard_map/while/body/eval_jaxpr/psum | solution.py:76
  1433.6 45.7 %psum.39 = bf16[64,256]{1,0:T(8,128)(2,1)S(1)} all-reduce(bf16[64,256]{1,0:T(8,128)(2,1)S(1)} %convolution_convert_fusion.6), channel_id=1, replica_groups=mesh['sub'=4,'row'=16,'col'=4] {'row'}, use_global_device_ids=true, to_apply=%region_5.5 | all-reduce | flops 16384 | bytes 65536 | tf_op jit(solution)/shard_map/while/body/eval_jaxpr/psum | solution.py:76
  1481.4 45.7 %psum.39 = bf16[64,256]{1,0:T(8,128)(2,1)S(1)} all-reduce(bf16[64,256]{1,0:T(8,128)(2,1)S(1)} %convolution_convert_fusion.6), channel_id=1, replica_groups=mesh['sub'=4,'row'=16,'col'=4] {'row'}, use_global_device_ids=true, to_apply=%region_5.5 | all-reduce | flops 16384 | bytes 65536 | tf_op jit(solution)/shard_map/while/body/eval_jaxpr/psum | solution.py:76
  1529.3 45.7 %psum.39 = bf16[64,256]{1,0:T(8,128)(2,1)S(1)} all-reduce(bf16[64,256]{1,0:T(8,128)(2,1)S(1)} %convolution_convert_fusion.6), channel_id=1, replica_groups=mesh['sub'=4,'row'=16,'col'=4] {'row'}, use_global_device_ids=true, to_apply=%region_5.5 | all-reduce | flops 16384 | bytes 65536 | tf_op jit(solution)/shard_map/while/body/eval_jaxpr/psum | solution.py:76
  1577.1 45.7 %psum.39 = bf16[64,256]{1,0:T(8,128)(2,1)S(1)} all-reduce(bf16[64,256]{1,0:T(8,128)(2,1)S(1)} %convolution_convert_fusion.6), channel_id=1, replica_groups=mesh['sub'=4,'row'=16,'col'=4] {'row'}, use_global_device_ids=true, to_apply=%region_5.5 | all-reduce | flops 16384 | bytes 65536 | tf_op jit(solution)/shard_map/while/body/eval_jaxpr/psum | solution.py:76
  1625.0 45.7 %psum.39 = bf16[64,256]{1,0:T(8,128)(2,1)S(1)} all-reduce(bf16[64,256]{1,0:T(8,128)(2,1)S(1)} %convolution_convert_fusion.6), channel_id=1, replica_groups=mesh['sub'=4,'row'=16,'col'=4] {'row'}, use_global_device_ids=true, to_apply=%region_5.5 | all-reduce | flops 16384 | bytes 65536 | tf_op jit(solution)/shard_map/while/body/eval_jaxpr/psum | solution.py:76
  1671.8 6.4 fusion.44
  1678.8 65.5 %reduce-scatter.2.cloned.1.call-done = bf16[4,64,256]{2,1,0:T(8,128)(2,1)} async-done(((bf16[64,64,256]{2,1,0:T(8,128)(2,1)}), bf16[4,64,256]{2,1,0:T(8,128)(2,1)}) %reduce-scatter.2.cloned.1.call-update) | async-done | bytes 131088 | tf_op jit(solution)/shard_map/reduce_scatter | solution.py:90
  1744.3 1.8 fusion.50
  (95 shorter events, 66.2 us)
Async XLA Ops:
  7.2 0.9 copy-start
  11.0 9.5 copy-start.2
  11.0 57.9 %all-to-all-start = ((bf16[16,4,64,256]{3,2,1,0:T(8,128)(2,1)}), bf16[16,4,64,256]{3,2,1,0:T(8,128)(2,1)S(1)}, u32[]{:S(2)}, u32[]{:S(2)}) async-start(bf16[16,4,64,256]{3,2,1,0:T(8,128)(2,1)} %stack.2), calls=%async_computation | async-start | bytes 4194304 | tf_op jit(solution)/shard_map/all_to_all | solution.py:28
  19.7 118.4 %all-gather.2.cloned.1.call-start = ((), (), s32[]{:S(2)}) async-start(), calls=%async_computation.2 | async-start | bytes 2621440 | tf_op jit(solution)/shard_map/all_gather | solution.py:37
  20.4 1723.9 %reduce-scatter.2.cloned.1.call-start = ((), (), s32[]{:S(2)}) async-start(), calls=%async_computation.3 | async-start | bytes 2228224 | tf_op jit(solution)/shard_map/reduce_scatter | solution.py:90
  1678.1 66.2 %copy-start.1 = (bf16[1,4,1,256,256]{4,3,2,1,0:T(8,128)(2,1)S(1)}, bf16[1,4,1,256,256]{4,3,2,1,0:T(8,128)(2,1)}, u32[]{:S(2)}) copy-start(bf16[1,4,1,256,256]{4,3,2,1,0:T(8,128)(2,1)} %param.12) | copy-start | bytes 1572868
Sparse Core Ops, SparseCore 0:
  22.3 34.9 all-gather.1
  1678.3 66.0 reduce-scatter.1
